TPU v7x, 128 devices: a whole 4x4x4 slice. The times are simulated.
128 devices in a mesh: view: 4 (over y), tile: 32 (over z, x, core).
Axes of the slice: x: 4, y: 4, z: 4, core: 2. Of those that a mesh axis runs over, the one named last changes fastest.
Arguments:
- estimate: float32 [128, 768, 512], P(None, 'tile'), may hold values from 0.5 to 2
- view_stacks: float32 [4, 128, 768, 512], P('view', 'tile'), may hold values from 0 to 4
- profile_z: float32 [4, 31], P('view'), may hold values from 0.2 to 1
- profile_y: float32 [4, 15], P('view'), may hold values from 0.2 to 1
- profile_x: float32 [4, 15], P('view'), may hold values from 0.2 to 1
- offsets: int32 [4], P('view'), may hold values from -16 to 16, as said below
- coverage: int32 [32, 4], P('tile'), may hold values from 0 to 1, as said below
Outputs:
- new_estimate: float32 [128, 768, 512], P(None, 'tile')
Inputs may be any that keep to these rules, and one draw needn't show every extreme that they name: `offsets`: some view has offset 16 and some view has offset -16. `coverage`: every tile is intersected by at least one view.
All inputs are finite; a program needn't handle non-finite values.
Results may differ from a plain program's by a relative error of at most 0.0001.
Values sent between devices are 32-bit elements; how exact they have to be, the bound alone decides.
A program may use at most 192 MiB of HBM per device.

v0:
```python
import jax
import jax.numpy as jnp
from jax import lax
from jax.sharding import PartitionSpec as P

MAXOFF = 16


def with_halo(cells, sides, width):
    for axis, dim in sides:
        count = lax.axis_size(axis)
        ends = count - 1
        head = lax.slice_in_dim(cells, 0, width, axis=dim)
        tail = lax.slice_in_dim(cells, cells.shape[dim] - width, cells.shape[dim], axis=dim)
        cells = jnp.concatenate(
            [
                lax.ppermute(tail, axis, [(i, (i + 1) % count) for i in range(ends)]),
                cells,
                lax.ppermute(head, axis, [((i + 1) % count, i) for i in range(ends)]),
            ],
            axis=dim,
        )
    return cells


def band_matrix(kernel, rows_out):
    taps_count = kernel.shape[0]
    rows_in = rows_out + taps_count - 1
    out_index = jnp.arange(rows_out, dtype=jnp.int32)
    in_index = jnp.arange(rows_in, dtype=jnp.int32)
    distance = in_index[None, :] - out_index[:, None]
    tap_index = jnp.arange(taps_count, dtype=jnp.int32)
    hits = (distance[None, :, :] == tap_index[:, None, None]).astype(jnp.float32)
    return jnp.sum(hits * kernel[:, None, None], axis=0)


def band_blur(field, kernel, along):
    highest = lax.Precision.HIGHEST
    taps_count = kernel.shape[0]
    half = (taps_count - 1) // 2
    extent = field.shape[along]
    block = min(128, extent)
    count = extent // block
    widths = [(0, 0), (0, 0), (0, 0)]
    widths[along] = (half, block - half)
    padded = jnp.pad(field, widths)
    band = band_matrix(kernel, block)
    head_band = band[:, :block]
    tail_band = band[:, block:]
    head = lax.slice_in_dim(padded, 0, count * block, axis=along)
    tail = lax.slice_in_dim(padded, block, (count + 1) * block, axis=along)
    if along == 0:
        head = head.reshape((count, block) + field.shape[1:])
        tail = tail.reshape((count, block) + field.shape[1:])[:, : taps_count - 1]
        result = jnp.einsum(
            "jbyx,ob->joyx", head, head_band, precision=highest, preferred_element_type=jnp.float32
        )
        result = result + jnp.einsum(
            "jbyx,ob->joyx", tail, tail_band, precision=highest, preferred_element_type=jnp.float32
        )
        return result.reshape(field.shape)
    head = head.reshape(field.shape[:2] + (count, block))
    tail = tail.reshape(field.shape[:2] + (count, block))[..., : taps_count - 1]
    result = jnp.einsum(
        "zyjb,ob->zyjo", head, head_band, precision=highest, preferred_element_type=jnp.float32
    )
    result = result + jnp.einsum(
        "zyjb,ob->zyjo", tail, tail_band, precision=highest, preferred_element_type=jnp.float32
    )
    return result.reshape(field.shape)


def blur_rows(field, matrix_y, weights_z, weights_x):
    highest = lax.Precision.HIGHEST
    result = band_blur(field, weights_z, 0)
    result = jnp.einsum(
        "ya,zax->zyx", matrix_y, result, precision=highest, preferred_element_type=jnp.float32
    )
    return band_blur(result, weights_x, 2)


def on_device(estimate, view_stacks, profile_z, profile_y, profile_x, offsets, coverage):
    weights_z = profile_z[0] / jnp.sum(profile_z[0])
    weights_y = profile_y[0] / jnp.sum(profile_y[0])
    weights_x = profile_x[0] / jnp.sum(profile_x[0])
    row_count = estimate.shape[1]
    x_cells = estimate.shape[2]
    half_y = (weights_y.shape[0] - 1) // 2
    padded = jnp.pad(view_stacks[0], ((0, 0), (0, 0), (MAXOFF, MAXOFF)))
    shifted = lax.dynamic_slice_in_dim(padded, MAXOFF + offsets[0], x_cells, 2)
    stacked = lax.all_to_all(shifted, "tile", split_axis=1, concat_axis=0, tiled=True)
    flipped = weights_y[::-1]
    back_z = weights_z[::-1]
    back_x = weights_x[::-1]
    estimate_ext = with_halo(estimate, (("tile", 1),), half_y)
    blurred = blur_rows(estimate_ext, band_matrix(weights_y, row_count), weights_z, weights_x)
    quotient = stacked / blurred
    quotient_ext = with_halo(quotient, (("tile", 1),), half_y)
    back_blur = blur_rows(quotient_ext, band_matrix(flipped, row_count), back_z, back_x)
    view_index = lax.axis_index("view")
    covered = lax.dynamic_index_in_dim(coverage[0], view_index, 0, keepdims=False).astype(
        jnp.float32
    )
    view_count = jnp.sum(coverage[0]).astype(jnp.float32)
    weighted = covered * back_blur
    summed = lax.psum(weighted, "view")
    return estimate * summed / view_count


def solution(mesh):
    return jax.shard_map(
        on_device,
        mesh=mesh,
        in_specs=(
            P(None, "tile", None),
            P("view", "tile", None, None),
            P("view", None),
            P("view", None),
            P("view", None),
            P("view"),
            P("tile", None),
        ),
        out_specs=P(None, "tile", None),
        check_vma=False,
    )
```

profile of v0, /device:TPU:1, one launch (start us, length us, event | category | flops | bytes accessed | tf_op | source)
XLA Modules:
  0.0 461.1 jit_solution(2243969198912554570)
XLA Ops:
  6.5 6.4 %copy.65 = f32[128,24,512]{2,0,1:T(8,128)S(1)} copy(f32[128,24,512]{2,1,0:T(8,128)} %param.7) | data formatting | bytes 12582912 | tf_op args[0]
  13.0 0.0 copy-start
  13.0 2.7 copy-done
  15.7 2.2 fusion.39
  17.9 4.7 %collective-permute-start = (f32[128,7,512]{2,0,1:T(8,128)}, f32[128,7,512]{2,0,1:T(8,128)S(1)}, u32[]{:S(2)}, u32[]{:S(2)}) collective-permute-start(f32[128,7,512]{2,0,1:T(8,128)} %get-tuple-element.17), channel_id=1, source_target_pairs={{0,1},{1,2},{2,3},{3,4},{4,5},{5,6},{6,7},{7,8},{8,9},{9,10},{10,1... | collective-permute-start | bytes 5505032 | tf_op jit(solution)/shard_map/ppermute | solution.py:17
  22.7 2.1 collective-permute-start.1
  25.4 6.7 %copy.107 = f32[1,4,768,512]{3,1,2,0:T(4,128)} copy(f32[1,4,768,512]{3,2,1,0:T(8,128)S(1)} %copy-done.4) | data formatting | bytes 12582912 | tf_op args[1]
  32.1 8.7 %pad_dynamic-slice_fusion = f32[4,768,512]{2,0,1:T(4,128)} fusion(s32[]{:T(128)S(6)} %select_n.8, f32[4,768,512]{2,0,1:T(4,128)} %bitcast.76), kind=kLoop, calls=%fused_computation.21 | loop fusion | bytes 12582916 | tf_op jit(solution)/shard_map/dynamic_slice | solution.py:90
  40.9 8.7 %all-to-all-start = ((f32[4,768,512]{2,0,1:T(4,128)}), f32[4,768,512]{2,0,1:T(4,128)}, u32[]{:S(2)}, u32[]{:S(2)}) async-start(f32[4,768,512]{2,0,1:T(4,128)} %pad_dynamic-slice_fusion), calls=%async_computation | async-start | bytes 12582912 | tf_op jit(solution)/shard_map/all_to_all | solution.py:91
  49.6 0.4 all-reduce.7.cloned.1.call-start
  50.1 0.6 reduce_sum.90
  50.7 0.1 reverse.9
  50.8 0.6 reduce_sum.93
  51.4 0.1 reverse.10
  51.5 0.6 reduce_sum.95
  52.1 0.1 reverse.11
  52.2 0.6 broadcast_divide_fusion.2
  52.8 0.1 select_reduce_fusion.4
  53.0 0.6 broadcast_divide_fusion
  53.5 0.3 select_reduce_fusion.2
  53.8 0.6 broadcast_divide_fusion.4
  54.4 0.6 select_reduce_fusion.1
  55.0 0.0 collective-permute-done
  55.0 0.0 collective-permute-done.1
  55.0 11.0 %select_maximum_fusion.2 = f32[256,38,512]{2,0,1:T(8,128)} fusion(f32[128,7,512]{2,0,1:T(8,128)} %collective-permute-done.1, f32[128,24,512]{2,0,1:T(8,128)} %copy-done, f32[128,7,512]{2,0,1:T(8,128)S(1)} %collective-permute-done), kind=kLoop, calls=%fused_computation.4 | loop fusion | flops 39845888 | bytes 29884416 | tf_op jit(solution)/shard_map/concatenate | solution.py:15
  66.0 9.5 %slice_bitcast_fusion.1 = f32[1,128,38,512]{3,1,2,0:T(8,128)} fusion(f32[256,38,512]{2,0,1:T(8,128)} %select_maximum_fusion.2), kind=kLoop, calls=%fused_computation.14 | loop fusion | bytes 19922944 | tf_op jit(solution)/shard_map/reshape | solution.py:54
  75.5 9.8 %fusion.31 = f32[128,38,512]{2,0,1:T(8,128)S(1)} fusion(f32[1,128,38,512]{3,1,2,0:T(8,128)} %slice_bitcast_fusion.1, f32[128,158]{0,1:T(8,128)S(1)} %get-tuple-element.6), kind=kOutput, calls=%fused_computation.41 | convolution fusion | flops 896532480 | bytes 12468224 | tf_op jit(solution)/shard_map/jbyx,ob->joyx/dot_general | solution.py:58
  85.3 15.1 %fusion.13 = f32[128,38,512]{2,0,1:T(8,128)S(1)} fusion(f32[128,38,512]{2,0,1:T(8,128)S(1)} %fusion.31, f32[256,38,512]{2,0,1:T(8,128)} %select_maximum_fusion.2, f32[128,158]{0,1:T(8,128)S(1)} %get-tuple-element.6), kind=kOutput, calls=%fused_computation.30 | convolution fusion | flops 3827695616 | bytes 29949952 | tf_op jit(solution)/shard_map/jbyx,ob->joyx/dot_general | solution.py:55
  100.4 18.2 %fusion.24 = f32[128,24,512]{2,1,0:T(8,128)S(1)} fusion(f32[128,38,512]{2,0,1:T(8,128)S(1)} %fusion.13, f32[24,38]{1,0:T(8,128)S(1)} %get-tuple-element.10), kind=kOutput, calls=%fused_computation.33 | convolution fusion | flops 717225984 | bytes 16256576 | tf_op jit(solution)/shard_map/ya,zax->zyx/dot_general | solution.py:76
  118.6 6.4 %pad_slice_fusion.3 = (f32[128,24,512]{2,1,0:T(8,128)}, f32[128,24,512]{2,1,0:T(8,128)}) fusion(f32[128,24,512]{2,1,0:T(8,128)S(1)} %fusion.24), kind=kLoop, calls=%fused_computation.20 | loop fusion | bytes 18874368 | tf_op jit(solution)/shard_map/slice | solution.py:50
  125.0 6.6 %copy.83 = f32[128,24,512]{0,2,1:T(8,128)} copy(f32[128,24,512]{2,1,0:T(8,128)} %get-tuple-element.16) | data formatting | bytes 12582912 | tf_op jit(solution)/shard_map/reshape | solution.py:63
  131.6 7.6 %reshape.113 = f32[128,24,4,128]{3,2,1,0:T(4,128)} reshape(f32[128,24,512]{2,1,0:T(8,128)} %get-tuple-element.15) | data formatting | bytes 12582912 | tf_op jit(solution)/shard_map/reshape | solution.py:62
  139.1 6.5 %fusion.34 = f32[128,24,4,128]{0,3,2,1:T(8,128)S(1)} fusion(f32[128,24,4,128]{0,3,2,1:T(8,128)} %bitcast.84, f32[128,142]{0,1:T(8,128)S(1)} %get-tuple-element.8), kind=kOutput, calls=%fused_computation.47 | convolution fusion | flops 264241152 | bytes 7086080 | tf_op jit(solution)/shard_map/zyjb,ob->zyjo/dot_general | solution.py:67
  145.6 10.5 %fusion.19 = f32[128,24,4,128]{0,3,2,1:T(8,128)} fusion(f32[128,24,4,128]{0,3,2,1:T(8,128)S(1)} %fusion.34, f32[128,24,4,128]{3,2,1,0:T(4,128)S(1)} %copy-done.3, f32[128,142]{0,1:T(8,128)S(1)} %get-tuple-element.8), kind=kOutput, calls=%fused_computation.32 | convolution fusion | flops 2417491968 | bytes 18939904 | tf_op jit(solution)/shard_map/zyjb,ob->zyjo/dot_general | solution.py:64
  156.1 6.6 %copy.73 = f32[128,24,512]{2,0,1:T(8,128)} copy(f32[128,24,512]{0,2,1:T(8,128)} %bitcast.81) | data formatting | bytes 12582912 | tf_op jit(solution)/shard_map/reshape | solution.py:70
  162.7 0.0 all-to-all-done
  162.7 5.0 %copy.62 = f32[4,768,512]{2,1,0:T(8,128)S(1)} copy(f32[4,768,512]{2,0,1:T(4,128)} %all-to-all-done) | data formatting | bytes 12582912 | tf_op jit(solution)/shard_map/all_to_all | solution.py:91
  167.6 0.0 slice-start.1
  167.6 1.0 copy.63
  168.7 0.5 slice-done.1
  169.2 4.2 copy_divide_fusion
  173.5 0.0 copy-start.1
  173.5 2.7 copy-done.1
  176.2 2.2 fusion.38
  178.3 3.5 collective-permute-start.2
  181.9 1.9 collective-permute-start.3
  183.8 0.6 fusion.40
  184.4 17.9 %collective-permute-done.2 = f32[128,7,512]{2,0,1:T(8,128)S(1)} collective-permute-done((f32[128,7,512]{2,0,1:T(8,128)}, f32[128,7,512]{2,0,1:T(8,128)S(1)}, u32[]{:S(2)}, u32[]{:S(2)}) %collective-permute-start.2) | collective-permute-done | bytes 1835040 | tf_op jit(solution)/shard_map/ppermute | solution.py:17
  202.3 4.4 collective-permute-done.3
  206.7 11.2 %select_maximum_fusion = f32[256,38,512]{2,0,1:T(8,128)} fusion(f32[128,7,512]{2,0,1:T(8,128)} %collective-permute-done.3, f32[128,24,512]{2,0,1:T(8,128)} %copy-done.1, f32[128,7,512]{2,0,1:T(8,128)S(1)} %collective-permute-done.2), kind=kLoop, calls=%fused_computation.2 | loop fusion | flops 39845888 | bytes 29884416 | tf_op jit(solution)/shard_map/concatenate | solution.py:15
  217.9 9.5 %slice_bitcast_fusion = f32[1,128,38,512]{3,1,2,0:T(8,128)} fusion(f32[256,38,512]{2,0,1:T(8,128)} %select_maximum_fusion), kind=kLoop, calls=%fused_computation.11 | loop fusion | bytes 19922944 | tf_op jit(solution)/shard_map/reshape | solution.py:54
  227.5 9.8 %fusion.30 = f32[128,38,512]{2,0,1:T(8,128)S(1)} fusion(f32[1,128,38,512]{3,1,2,0:T(8,128)} %slice_bitcast_fusion, f32[128,158]{0,1:T(8,128)S(1)} %get-tuple-element.5), kind=kOutput, calls=%fused_computation.39 | convolution fusion | flops 896532480 | bytes 12468224 | tf_op jit(solution)/shard_map/jbyx,ob->joyx/dot_general | solution.py:58
  237.2 15.5 %fusion.16 = f32[128,38,512]{2,0,1:T(8,128)S(1)} fusion(f32[128,38,512]{2,0,1:T(8,128)S(1)} %fusion.30, f32[256,38,512]{2,0,1:T(8,128)} %select_maximum_fusion, f32[128,158]{0,1:T(8,128)S(1)} %get-tuple-element.5), kind=kOutput, calls=%fused_computation.31 | convolution fusion | flops 3827695616 | bytes 29949952 | tf_op jit(solution)/shard_map/jbyx,ob->joyx/dot_general | solution.py:55
  252.7 18.0 %fusion.27 = f32[128,24,512]{2,1,0:T(8,128)S(1)} fusion(f32[128,38,512]{2,0,1:T(8,128)S(1)} %fusion.16, f32[24,38]{1,0:T(8,128)S(1)} %get-tuple-element.9), kind=kOutput, calls=%fused_computation.34 | convolution fusion | flops 717225984 | bytes 16256576 | tf_op jit(solution)/shard_map/ya,zax->zyx/dot_general | solution.py:76
  270.8 6.4 %pad_slice_fusion.1 = (f32[128,24,512]{2,1,0:T(8,128)}, f32[128,24,512]{2,1,0:T(8,128)}) fusion(f32[128,24,512]{2,1,0:T(8,128)S(1)} %fusion.27), kind=kLoop, calls=%fused_computation.18 | loop fusion | bytes 18874368 | tf_op jit(solution)/shard_map/slice | solution.py:50
  277.2 6.6 %copy.84 = f32[128,24,512]{0,2,1:T(8,128)} copy(f32[128,24,512]{2,1,0:T(8,128)} %get-tuple-element.12) | data formatting | bytes 12582912 | tf_op jit(solution)/shard_map/reshape | solution.py:63
  283.7 7.6 %reshape.118 = f32[128,24,4,128]{3,2,1,0:T(4,128)} reshape(f32[128,24,512]{2,1,0:T(8,128)} %get-tuple-element.11) | data formatting | bytes 12582912 | tf_op jit(solution)/shard_map/reshape | solution.py:62
  291.3 6.5 %fusion.32 = f32[128,24,4,128]{0,3,2,1:T(8,128)S(1)} fusion(f32[128,24,4,128]{0,3,2,1:T(8,128)} %bitcast.83, f32[128,142]{0,1:T(8,128)S(1)} %get-tuple-element.7), kind=kOutput, calls=%fused_computation.45 | convolution fusion | flops 264241152 | bytes 7086080 | tf_op jit(solution)/shard_map/zyjb,ob->zyjo/dot_general | solution.py:67
  297.8 11.4 %add_multiply_fusion = f32[128,24,4,128]{0,3,2,1:T(8,128)} fusion(f32[128,24,4,128]{0,3,2,1:T(8,128)S(1)} %fusion.32, f32[]{:T(128)} %bitcast, f32[128,24,4,128]{3,2,1,0:T(4,128)S(1)} %copy-done.2, f32[128,142]{0,1:T(8,128)S(1)} %get-tuple-element.7), kind=kOutput, calls=%fused_computation.29 | convolution fusion | flops 2419064832 | bytes 18939908 | tf_op jit(solution)/shard_map/zyjb,ob->zyjo/dot_general | solution.py:64
  309.2 6.7 %copy.78 = f32[128,24,512]{2,1,0:T(8,128)} copy(f32[128,24,512]{0,2,1:T(8,128)} %bitcast.80) | data formatting | bytes 12582912 | tf_op jit(solution)/shard_map/mul | solution.py:105
  315.9 0.0 all-reduce.7.cloned.1.call-update
  315.9 0.6 reduce_sum.99
  317.2 127.9 %all-reduce.7.cloned.1.call-done = f32[128,24,512]{2,1,0:T(8,128)} async-done(((f32[128,24,512]{2,1,0:T(8,128)}), f32[128,24,512]{2,1,0:T(8,128)}) %all-reduce.7.cloned.1.call-update) | async-done | bytes 6291472 | tf_op jit(solution)/shard_map/psum | solution.py:106
  445.1 8.9 %multiply_divide_fusion = f32[128,24,512]{2,1,0:T(8,128)} fusion(f32[128,24,512]{2,1,0:T(8,128)} %param.7, f32[128,24,512]{2,1,0:T(8,128)} %all-reduce.7.cloned.1.call-done, f32[]{:T(128)S(6)} %convert_element_type.25), kind=kLoop, calls=%fused_computation.28 | loop fusion | flops 3145728 | bytes 18874372 | tf_op jit(solution)/shard_map/div | solution.py:107
  (20 shorter events, 0.1 us)
Async XLA Ops:
  13.0 2.7 copy-start
  15.7 9.8 %copy-start.4 = (f32[1,4,768,512]{3,2,1,0:T(8,128)S(1)}, f32[1,4,768,512]{3,2,1,0:T(8,128)}, u32[]{:S(2)}) copy-start(f32[1,4,768,512]{3,2,1,0:T(8,128)} %param.8) | copy-start | bytes 18874372
  17.9 37.0 %collective-permute-start = (f32[128,7,512]{2,0,1:T(8,128)}, f32[128,7,512]{2,0,1:T(8,128)S(1)}, u32[]{:S(2)}, u32[]{:S(2)}) collective-permute-start(f32[128,7,512]{2,0,1:T(8,128)} %get-tuple-element.17), channel_id=1, source_target_pairs={{0,1},{1,2},{2,3},{3,4},{4,5},{5,6},{6,7},{7,8},{8,9},{9,10},{10,1... | collective-permute-start | bytes 5505032 | tf_op jit(solution)/shard_map/ppermute | solution.py:17
  22.7 32.3 %collective-permute-start.1 = (f32[128,7,512]{2,0,1:T(8,128)}, f32[128,7,512]{2,0,1:T(8,128)}, u32[]{:S(2)}, u32[]{:S(2)}) collective-permute-start(f32[128,7,512]{2,0,1:T(8,128)} %get-tuple-element.18), channel_id=1, source_target_pairs={{1,0},{2,1},{3,2},{4,3},{5,4},{6,5},{7,6},{8,7},{9,8},{10,9},{11,1... | collective-permute-start | bytes 5505032 | tf_op jit(solution)/shard_map/ppermute | solution.py:19
  40.9 9.2 %copy-start.7 = (f32[1,31]{1,0:T(1,128)S(1)}, f32[1,31]{1,0:T(1,128)}, u32[]{:S(2)}) copy-start(f32[1,31]{1,0:T(1,128)} %param.9) | copy-start | bytes 376
  40.9 9.9 %copy-start.5 = (f32[1,15]{1,0:T(1,128)S(1)}, f32[1,15]{1,0:T(1,128)}, u32[]{:S(2)}) copy-start(f32[1,15]{1,0:T(1,128)} %param.10) | copy-start | bytes 184
  40.9 10.6 %copy-start.6 = (f32[1,15]{1,0:T(1,128)S(1)}, f32[1,15]{1,0:T(1,128)}, u32[]{:S(2)}) copy-start(f32[1,15]{1,0:T(1,128)} %param.11) | copy-start | bytes 184
  40.9 121.8 %all-to-all-start = ((f32[4,768,512]{2,0,1:T(4,128)}), f32[4,768,512]{2,0,1:T(4,128)}, u32[]{:S(2)}, u32[]{:S(2)}) async-start(f32[4,768,512]{2,0,1:T(4,128)} %pad_dynamic-slice_fusion), calls=%async_computation | async-start | bytes 12582912 | tf_op jit(solution)/shard_map/all_to_all | solution.py:91
  49.6 395.5 %all-reduce.7.cloned.1.call-start = ((), (), s32[]{:S(2)}) async-start(), calls=%async_computation.1 | async-start | bytes 12582912 | tf_op jit(solution)/shard_map/psum | solution.py:106
  139.1 6.5 %copy-start.3 = (f32[128,24,4,128]{3,2,1,0:T(4,128)S(1)}, f32[128,24,4,128]{3,2,1,0:T(4,128)}, u32[]{:S(2)}) copy-start(f32[128,24,4,128]{3,2,1,0:T(4,128)} %reshape.113) | copy-start | bytes 18874372
  162.7 6.0 %slice-start = ((s8[6291456]{0:T(1024)(128)(4,1)}), s8[4194304]{0:T(1024)(128)(4,1)S(1)}, s32[]{:S(2)}) async-start(s8[6291456]{0:T(1024)(128)(4,1)} %bitcast.78), calls=%async_computation.2 | async-start | bytes 8388608
  167.6 1.6 slice-start.1
  173.5 2.7 copy-start.1
  176.2 7.6 %copy-start.8 = (s32[1,4]{1,0:T(1,128)S(1)}, s32[1,4]{1,0:T(1,128)}, u32[]{:S(2)}) copy-start(s32[1,4]{1,0:T(1,128)} %param.13) | copy-start | bytes 52
  178.3 24.0 %collective-permute-start.2 = (f32[128,7,512]{2,0,1:T(8,128)}, f32[128,7,512]{2,0,1:T(8,128)S(1)}, u32[]{:S(2)}, u32[]{:S(2)}) collective-permute-start(f32[128,7,512]{2,0,1:T(8,128)} %get-tuple-element.13), channel_id=1, source_target_pairs={{0,1},{1,2},{2,3},{3,4},{4,5},{5,6},{6,7},{7,8},{8,9},{9,10},{10,1... | collective-permute-start | bytes 5505032 | tf_op jit(solution)/shard_map/ppermute | solution.py:17
  181.9 24.9 %collective-permute-start.3 = (f32[128,7,512]{2,0,1:T(8,128)}, f32[128,7,512]{2,0,1:T(8,128)}, u32[]{:S(2)}, u32[]{:S(2)}) collective-permute-start(f32[128,7,512]{2,0,1:T(8,128)} %get-tuple-element.14), channel_id=1, source_target_pairs={{1,0},{2,1},{3,2},{4,3},{5,4},{6,5},{7,6},{8,7},{9,8},{10,9},{11,1... | collective-permute-start | bytes 5505032 | tf_op jit(solution)/shard_map/ppermute | solution.py:19
  291.3 6.5 %copy-start.2 = (f32[128,24,4,128]{3,2,1,0:T(4,128)S(1)}, f32[128,24,4,128]{3,2,1,0:T(4,128)}, u32[]{:S(2)}) copy-start(f32[128,24,4,128]{3,2,1,0:T(4,128)} %reshape.118) | copy-start | bytes 18874372
Sparse Core Ops, SparseCore 0:
  316.0 129.0 all-reduce.6
where the time goes:
time: 466 us; the launch traced here: 461 us
  waiting for transfers between devices  150 us (32%)
  matrix products  121 us (26%)
  local copies, waits for them, and re-layouts  112 us (24%)
  other arithmetic  41 us (9%)
  starting transfers between devices  21.5 us (5%)
  between operations  15.2 us (3%)
    psum x1, waiting for transfers between devices, on_device(): summed = lax.psum(weighted, 'view')  128 us
    dot_general x2, matrix products, blur_rows(): jnp.einsum('ya,zax->zyx', matrix_y, result, precision=highest, preferred_...  36.2 us
    dot_general x2, matrix products, band_blur(): jnp.einsum('jbyx,ob->joyx', head, head_band, precision=highest, preferred...  30.6 us
    concatenate x2, other arithmetic, with_halo(): jnp.concatenate([lax.ppermute(tail, axis, [(i, (i + 1) % count) for i in...  22.2 us
    dot_general x2, matrix products, band_blur(): jnp.einsum('zyjb,ob->zyjo', head, head_band, precision=highest, preferred...  21.9 us
    dot_general x2, matrix products, band_blur(): jnp.einsum('jbyx,ob->joyx', tail, tail_band, precision=highest, preferred...  19.5 us
    reshape x2, local copies, waits for them, and re-layouts, band_blur(): tail = tail.reshape((count, block) + field.shape[1:])[:, :taps_count - 1]  19.1 us
    unnamed x24, local copies, waits for them, and re-layouts  19.1 us
  transfers between devices with their start and end apart: 6, of which 3 were waited for; matrix products, arithmetic and copies ran while one was open for 28% of the time, Pallas kernels for 0%

commit v1 on v0

--- a/solution.py
+++ b/solution.py
@@ -103,7 +103,7 @@
     )
     view_count = jnp.sum(coverage[0]).astype(jnp.float32)
     weighted = covered * back_blur
-    summed = lax.psum(weighted, "view")
+    summed = lax.all_gather(weighted, "view").sum(axis=0)
     return estimate * summed / view_count
 
 

time: 466 us -> 589 us (1.26)
  waiting for transfers between devices: 150 us -> 240 us
  local copies, waits for them, and re-layouts: 112 us -> 132 us
  other arithmetic: 41 us -> 53.6 us
    all_gather x0 -> x1, waiting for transfers between devices: none -> 218 us  [on_device(): summed = lax.all_gather(weighted, 'view').sum(axis=0)]
    psum x1 -> x0, waiting for transfers between devices: 128 us -> none  [on_device(): summed = lax.psum(weighted, 'view')]
    reduce_sum x0 -> x1, other arithmetic: none -> 13.2 us  [on_device(): summed = lax.all_gather(weighted, 'view').sum(axis=0)]
    unnamed x24 -> x26, local copies, waits for them, and re-layouts: 19.1 us -> 32.2 us
    div x0 -> x1, local copies, waits for them, and re-layouts: none -> 6.57 us  [on_device(): return estimate * summed / view_count]
  transfers between devices with their start and end apart: 6 -> 6, of which waited for: 3 -> 3; matrix products, arithmetic and copies ran while one was open for 28% -> 23% of each run, Pallas kernels for 0% -> 0%
where the time goes in v1:
time: 589 us; the launch traced here: 584 us
  waiting for transfers between devices  240 us (41%)
  local copies, waits for them, and re-layouts  132 us (22%)
  matrix products  121 us (21%)
  other arithmetic  53.6 us (9%)
  starting transfers between devices  21.6 us (4%)
  between operations  15.5 us (3%)
    all_gather x1, waiting for transfers between devices, on_device(): summed = lax.all_gather(weighted, 'view').sum(axis=0)  218 us
    dot_general x2, matrix products, blur_rows(): jnp.einsum('ya,zax->zyx', matrix_y, result, precision=highest, preferred_...  36.2 us
    unnamed x26, local copies, waits for them, and re-layouts  32.2 us
    dot_general x2, matrix products, band_blur(): jnp.einsum('jbyx,ob->joyx', head, head_band, precision=highest, preferred...  30.6 us
    concatenate x2, other arithmetic, with_halo(): jnp.concatenate([lax.ppermute(tail, axis, [(i, (i + 1) % count) for i in...  22.2 us
    dot_general x2, matrix products, band_blur(): jnp.einsum('zyjb,ob->zyjo', head, head_band, precision=highest, preferred...  21.9 us
    dot_general x2, matrix products, band_blur(): jnp.einsum('jbyx,ob->joyx', tail, tail_band, precision=highest, preferred...  19.5 us
    reshape x2, local copies, waits for them, and re-layouts, band_blur(): tail = tail.reshape((count, block) + field.shape[1:])[:, :taps_count - 1]  19.1 us
  transfers between devices with their start and end apart: 6, of which 3 were waited for; matrix products, arithmetic and copies ran while one was open for 23% of the time, Pallas kernels for 0%

profile of v1, /device:TPU:1, one launch (start us, length us, event | category | flops | bytes accessed | tf_op | source)
XLA Modules:
  0.0 583.9 jit_solution(7412942745128743058)
XLA Ops:
  6.5 6.4 %copy.65 = f32[128,24,512]{2,0,1:T(8,128)S(1)} copy(f32[128,24,512]{2,1,0:T(8,128)} %param.7) | data formatting | bytes 12582912 | tf_op args[0]
  13.0 0.0 copy-start
  13.0 2.7 copy-done
  15.7 2.2 fusion.39
  17.9 4.7 collective-permute-start
  22.7 2.1 collective-permute-start.1
  25.5 6.7 %copy.111 = f32[1,4,768,512]{3,1,2,0:T(4,128)} copy(f32[1,4,768,512]{3,2,1,0:T(8,128)S(1)} %copy-done.4) | data formatting | bytes 12582912 | tf_op args[1]
  32.2 8.7 %pad_dynamic-slice_fusion = f32[4,768,512]{2,0,1:T(4,128)} fusion(s32[]{:T(128)S(6)} %select_n.8, f32[4,768,512]{2,0,1:T(4,128)} %bitcast.76), kind=kLoop, calls=%fused_computation.21 | loop fusion | bytes 12582916 | tf_op jit(solution)/shard_map/dynamic_slice | solution.py:90
  40.9 8.7 %all-to-all-start = ((f32[4,768,512]{2,0,1:T(4,128)}), f32[4,768,512]{2,0,1:T(4,128)}, u32[]{:S(2)}, u32[]{:S(2)}) async-start(f32[4,768,512]{2,0,1:T(4,128)} %pad_dynamic-slice_fusion), calls=%async_computation | async-start | bytes 12582912 | tf_op jit(solution)/shard_map/all_to_all | solution.py:91
  49.7 0.5 all-gather.2.cloned.1.call-start
  50.2 0.6 reduce_sum.99
  50.8 0.1 reverse.9
  50.9 0.6 reduce_sum.102
  51.5 0.1 reverse.10
  51.6 0.6 reduce_sum.104
  52.2 0.1 reverse.11
  52.3 0.6 broadcast_divide_fusion.2
  52.9 0.1 select_reduce_fusion.4
  53.1 0.6 broadcast_divide_fusion
  53.6 0.3 select_reduce_fusion.2
  53.9 0.6 broadcast_divide_fusion.4
  54.5 0.6 select_reduce_fusion.1
  55.1 11.0 %select_maximum_fusion.2 = f32[256,38,512]{2,0,1:T(8,128)} fusion(f32[128,7,512]{2,0,1:T(8,128)} %collective-permute-done.1, f32[128,24,512]{2,0,1:T(8,128)} %copy-done, f32[128,7,512]{2,0,1:T(8,128)S(1)} %collective-permute-done), kind=kLoop, calls=%fused_computation.4 | loop fusion | flops 39845888 | bytes 29884416 | tf_op jit(solution)/shard_map/concatenate | solution.py:15
  66.1 9.5 %slice_bitcast_fusion.1 = f32[1,128,38,512]{3,1,2,0:T(8,128)} fusion(f32[256,38,512]{2,0,1:T(8,128)} %select_maximum_fusion.2), kind=kLoop, calls=%fused_computation.14 | loop fusion | bytes 19922944 | tf_op jit(solution)/shard_map/reshape | solution.py:54
  75.6 9.8 %fusion.31 = f32[128,38,512]{2,0,1:T(8,128)S(1)} fusion(f32[1,128,38,512]{3,1,2,0:T(8,128)} %slice_bitcast_fusion.1, f32[128,158]{0,1:T(8,128)S(1)} %get-tuple-element.6), kind=kOutput, calls=%fused_computation.41 | convolution fusion | flops 896532480 | bytes 12468224 | tf_op jit(solution)/shard_map/jbyx,ob->joyx/dot_general | solution.py:58
  85.4 15.1 %fusion.13 = f32[128,38,512]{2,0,1:T(8,128)S(1)} fusion(f32[128,38,512]{2,0,1:T(8,128)S(1)} %fusion.31, f32[256,38,512]{2,0,1:T(8,128)} %select_maximum_fusion.2, f32[128,158]{0,1:T(8,128)S(1)} %get-tuple-element.6), kind=kOutput, calls=%fused_computation.30 | convolution fusion | flops 3827695616 | bytes 29949952 | tf_op jit(solution)/shard_map/jbyx,ob->joyx/dot_general | solution.py:55
  100.5 18.2 %fusion.24 = f32[128,24,512]{2,1,0:T(8,128)S(1)} fusion(f32[128,38,512]{2,0,1:T(8,128)S(1)} %fusion.13, f32[24,38]{1,0:T(8,128)S(1)} %get-tuple-element.10), kind=kOutput, calls=%fused_computation.33 | convolution fusion | flops 717225984 | bytes 16256576 | tf_op jit(solution)/shard_map/ya,zax->zyx/dot_general | solution.py:76
  118.7 6.4 %pad_slice_fusion.3 = (f32[128,24,512]{2,1,0:T(8,128)}, f32[128,24,512]{2,1,0:T(8,128)}) fusion(f32[128,24,512]{2,1,0:T(8,128)S(1)} %fusion.24), kind=kLoop, calls=%fused_computation.20 | loop fusion | bytes 18874368 | tf_op jit(solution)/shard_map/slice | solution.py:50
  125.1 6.6 %copy.86 = f32[128,24,512]{0,2,1:T(8,128)} copy(f32[128,24,512]{2,1,0:T(8,128)} %get-tuple-element.16) | data formatting | bytes 12582912 | tf_op jit(solution)/shard_map/reshape | solution.py:63
  131.7 7.6 %reshape.123 = f32[128,24,4,128]{3,2,1,0:T(4,128)} reshape(f32[128,24,512]{2,1,0:T(8,128)} %get-tuple-element.15) | data formatting | bytes 12582912 | tf_op jit(solution)/shard_map/reshape | solution.py:62
  139.2 6.5 %fusion.34 = f32[128,24,4,128]{0,3,2,1:T(8,128)S(1)} fusion(f32[128,24,4,128]{0,3,2,1:T(8,128)} %bitcast.84, f32[128,142]{0,1:T(8,128)S(1)} %get-tuple-element.8), kind=kOutput, calls=%fused_computation.47 | convolution fusion | flops 264241152 | bytes 7086080 | tf_op jit(solution)/shard_map/zyjb,ob->zyjo/dot_general | solution.py:67
  145.7 10.5 %fusion.19 = f32[128,24,4,128]{0,3,2,1:T(8,128)} fusion(f32[128,24,4,128]{0,3,2,1:T(8,128)S(1)} %fusion.34, f32[128,24,4,128]{3,2,1,0:T(4,128)S(1)} %copy-done.3, f32[128,142]{0,1:T(8,128)S(1)} %get-tuple-element.8), kind=kOutput, calls=%fused_computation.32 | convolution fusion | flops 2417491968 | bytes 18939904 | tf_op jit(solution)/shard_map/zyjb,ob->zyjo/dot_general | solution.py:64
  156.2 6.6 %copy.73 = f32[128,24,512]{2,0,1:T(8,128)} copy(f32[128,24,512]{0,2,1:T(8,128)} %bitcast.81) | data formatting | bytes 12582912 | tf_op jit(solution)/shard_map/reshape | solution.py:70
  162.8 5.0 copy.62
  167.7 1.0 copy.63
  168.8 0.5 slice-done.1
  169.3 4.2 copy_divide_fusion
  173.6 0.0 copy-start.1
  173.6 2.7 copy-done.1
  176.3 2.2 fusion.38
  178.4 3.5 collective-permute-start.2
  182.0 1.9 collective-permute-start.3
  183.9 0.6 fusion.40
  184.5 17.9 %collective-permute-done.2 = f32[128,7,512]{2,0,1:T(8,128)S(1)} collective-permute-done((f32[128,7,512]{2,0,1:T(8,128)}, f32[128,7,512]{2,0,1:T(8,128)S(1)}, u32[]{:S(2)}, u32[]{:S(2)}) %collective-permute-start.2) | collective-permute-done | bytes 1835040 | tf_op jit(solution)/shard_map/ppermute | solution.py:17
  202.4 4.4 collective-permute-done.3
  206.8 11.2 %select_maximum_fusion = f32[256,38,512]{2,0,1:T(8,128)} fusion(f32[128,7,512]{2,0,1:T(8,128)} %collective-permute-done.3, f32[128,24,512]{2,0,1:T(8,128)} %copy-done.1, f32[128,7,512]{2,0,1:T(8,128)S(1)} %collective-permute-done.2), kind=kLoop, calls=%fused_computation.2 | loop fusion | flops 39845888 | bytes 29884416 | tf_op jit(solution)/shard_map/concatenate | solution.py:15
  218.0 9.5 %slice_bitcast_fusion = f32[1,128,38,512]{3,1,2,0:T(8,128)} fusion(f32[256,38,512]{2,0,1:T(8,128)} %select_maximum_fusion), kind=kLoop, calls=%fused_computation.11 | loop fusion | bytes 19922944 | tf_op jit(solution)/shard_map/reshape | solution.py:54
  227.6 9.8 %fusion.30 = f32[128,38,512]{2,0,1:T(8,128)S(1)} fusion(f32[1,128,38,512]{3,1,2,0:T(8,128)} %slice_bitcast_fusion, f32[128,158]{0,1:T(8,128)S(1)} %get-tuple-element.5), kind=kOutput, calls=%fused_computation.39 | convolution fusion | flops 896532480 | bytes 12468224 | tf_op jit(solution)/shard_map/jbyx,ob->joyx/dot_general | solution.py:58
  237.3 15.5 %fusion.16 = f32[128,38,512]{2,0,1:T(8,128)S(1)} fusion(f32[128,38,512]{2,0,1:T(8,128)S(1)} %fusion.30, f32[256,38,512]{2,0,1:T(8,128)} %select_maximum_fusion, f32[128,158]{0,1:T(8,128)S(1)} %get-tuple-element.5), kind=kOutput, calls=%fused_computation.31 | convolution fusion | flops 3827695616 | bytes 29949952 | tf_op jit(solution)/shard_map/jbyx,ob->joyx/dot_general | solution.py:55
  252.8 18.0 %fusion.27 = f32[128,24,512]{2,1,0:T(8,128)S(1)} fusion(f32[128,38,512]{2,0,1:T(8,128)S(1)} %fusion.16, f32[24,38]{1,0:T(8,128)S(1)} %get-tuple-element.9), kind=kOutput, calls=%fused_computation.34 | convolution fusion | flops 717225984 | bytes 16256576 | tf_op jit(solution)/shard_map/ya,zax->zyx/dot_general | solution.py:76
  270.9 6.4 %pad_slice_fusion.1 = (f32[128,24,512]{2,1,0:T(8,128)}, f32[128,24,512]{2,1,0:T(8,128)}) fusion(f32[128,24,512]{2,1,0:T(8,128)S(1)} %fusion.27), kind=kLoop, calls=%fused_computation.18 | loop fusion | bytes 18874368 | tf_op jit(solution)/shard_map/slice | solution.py:50
  277.3 6.6 %copy.87 = f32[128,24,512]{0,2,1:T(8,128)} copy(f32[128,24,512]{2,1,0:T(8,128)} %get-tuple-element.12) | data formatting | bytes 12582912 | tf_op jit(solution)/shard_map/reshape | solution.py:63
  283.8 7.6 %reshape.128 = f32[128,24,4,128]{3,2,1,0:T(4,128)} reshape(f32[128,24,512]{2,1,0:T(8,128)} %get-tuple-element.11) | data formatting | bytes 12582912 | tf_op jit(solution)/shard_map/reshape | solution.py:62
  291.4 6.5 %fusion.32 = f32[128,24,4,128]{0,3,2,1:T(8,128)S(1)} fusion(f32[128,24,4,128]{0,3,2,1:T(8,128)} %bitcast.83, f32[128,142]{0,1:T(8,128)S(1)} %get-tuple-element.7), kind=kOutput, calls=%fused_computation.45 | convolution fusion | flops 264241152 | bytes 7086080 | tf_op jit(solution)/shard_map/zyjb,ob->zyjo/dot_general | solution.py:67
  297.9 11.4 %add_multiply_fusion = f32[128,24,4,128]{0,3,2,1:T(8,128)} fusion(f32[128,24,4,128]{0,3,2,1:T(8,128)S(1)} %fusion.32, f32[]{:T(128)} %bitcast, f32[128,24,4,128]{3,2,1,0:T(4,128)S(1)} %copy-done.2, f32[128,142]{0,1:T(8,128)S(1)} %get-tuple-element.7), kind=kOutput, calls=%fused_computation.29 | convolution fusion | flops 2419064832 | bytes 18939908 | tf_op jit(solution)/shard_map/zyjb,ob->zyjo/dot_general | solution.py:64
  309.3 6.7 %copy.78 = f32[1,128,24,512]{3,2,1,0:T(8,128)} copy(f32[1,128,24,512]{1,3,2,0:T(8,128)} %bitcast.80) | data formatting | bytes 12582912 | tf_op jit(solution)/shard_map/mul | solution.py:105
  315.9 0.0 all-gather.2.cloned.1.call-update
  316.0 6.6 %copy.80 = f32[128,24,512]{0,2,1:T(8,128)} copy(f32[128,24,512]{2,1,0:T(8,128)} %param.7) | data formatting | bytes 12582912 | tf_op args[0]
  322.5 0.7 reduce_sum.109
  324.0 218.1 %all-gather.2.cloned.1.call-done = f32[4,128,24,512]{3,2,1,0:T(8,128)} async-done(((f32[1,128,24,512]{3,2,1,0:T(8,128)}), f32[4,128,24,512]{3,2,1,0:T(8,128)}) %all-gather.2.cloned.1.call-update) | async-done | bytes 25165840 | tf_op jit(solution)/shard_map/all_gather | solution.py:106
  542.1 13.2 %reduce_sum.108 = f32[128,24,512]{2,1,0:T(8,128)} reduce(f32[4,128,24,512]{3,2,1,0:T(8,128)} %all-gather.2.cloned.1.call-done, f32[]{:T(128)} %constant.27.clone.1), dimensions={0}, to_apply=%region_9.10 | reduce | flops 4718592 | bytes 31457284 | tf_op jit(solution)/shard_map/reduce_sum | solution.py:106
  555.3 6.5 %copy.88 = f32[128,24,512]{0,2,1:T(8,128)} copy(f32[128,24,512]{2,1,0:T(8,128)} %reduce_sum.108) | data formatting | bytes 12582912
  561.8 8.2 %multiply_divide_fusion = f32[128,24,512]{0,2,1:T(8,128)} fusion(f32[128,24,512]{0,2,1:T(8,128)} %copy.80, f32[128,24,512]{0,2,1:T(8,128)} %copy.88, f32[]{:T(128)S(6)} %convert_element_type.25), kind=kLoop, calls=%fused_computation.28 | loop fusion | flops 3145728 | bytes 18874372 | tf_op jit(solution)/shard_map/div | solution.py:107
  570.0 6.6 %copy.81 = f32[128,24,512]{2,1,0:T(8,128)} copy(f32[128,24,512]{0,2,1:T(8,128)} %multiply_divide_fusion) | data formatting | bytes 12582912 | tf_op jit(solution)/shard_map/div | solution.py:107
  (24 shorter events, 0.1 us)
Async XLA Ops:
  13.0 2.7 copy-start
  15.7 9.8 %copy-start.4 = (f32[1,4,768,512]{3,2,1,0:T(8,128)S(1)}, f32[1,4,768,512]{3,2,1,0:T(8,128)}, u32[]{:S(2)}) copy-start(f32[1,4,768,512]{3,2,1,0:T(8,128)} %param.8) | copy-start | bytes 18874372
  17.9 37.1 %collective-permute-start = (f32[128,7,512]{2,0,1:T(8,128)}, f32[128,7,512]{2,0,1:T(8,128)S(1)}, u32[]{:S(2)}, u32[]{:S(2)}) collective-permute-start(f32[128,7,512]{2,0,1:T(8,128)} %get-tuple-element.17), channel_id=1, source_target_pairs={{0,1},{1,2},{2,3},{3,4},{4,5},{5,6},{6,7},{7,8},{8,9},{9,10},{10,1... | collective-permute-start | bytes 5505032 | tf_op jit(solution)/shard_map/ppermute | solution.py:17
  22.7 32.4 %collective-permute-start.1 = (f32[128,7,512]{2,0,1:T(8,128)}, f32[128,7,512]{2,0,1:T(8,128)}, u32[]{:S(2)}, u32[]{:S(2)}) collective-permute-start(f32[128,7,512]{2,0,1:T(8,128)} %get-tuple-element.18), channel_id=1, source_target_pairs={{1,0},{2,1},{3,2},{4,3},{5,4},{6,5},{7,6},{8,7},{9,8},{10,9},{11,1... | collective-permute-start | bytes 5505032 | tf_op jit(solution)/shard_map/ppermute | solution.py:19
  40.9 9.3 %copy-start.7 = (f32[1,31]{1,0:T(1,128)S(1)}, f32[1,31]{1,0:T(1,128)}, u32[]{:S(2)}) copy-start(f32[1,31]{1,0:T(1,128)} %param.9) | copy-start | bytes 376
  40.9 10.0 %copy-start.5 = (f32[1,15]{1,0:T(1,128)S(1)}, f32[1,15]{1,0:T(1,128)}, u32[]{:S(2)}) copy-start(f32[1,15]{1,0:T(1,128)} %param.10) | copy-start | bytes 184
  40.9 10.7 %copy-start.6 = (f32[1,15]{1,0:T(1,128)S(1)}, f32[1,15]{1,0:T(1,128)}, u32[]{:S(2)}) copy-start(f32[1,15]{1,0:T(1,128)} %param.11) | copy-start | bytes 184
  40.9 121.9 %all-to-all-start = ((f32[4,768,512]{2,0,1:T(4,128)}), f32[4,768,512]{2,0,1:T(4,128)}, u32[]{:S(2)}, u32[]{:S(2)}) async-start(f32[4,768,512]{2,0,1:T(4,128)} %pad_dynamic-slice_fusion), calls=%async_computation | async-start | bytes 12582912 | tf_op jit(solution)/shard_map/all_to_all | solution.py:91
  49.7 492.4 %all-gather.2.cloned.1.call-start = ((), (), s32[]{:S(2)}) async-start(), calls=%async_computation.1 | async-start | bytes 31457280 | tf_op jit(solution)/shard_map/all_gather | solution.py:106
  139.2 6.5 %copy-start.3 = (f32[128,24,4,128]{3,2,1,0:T(4,128)S(1)}, f32[128,24,4,128]{3,2,1,0:T(4,128)}, u32[]{:S(2)}) copy-start(f32[128,24,4,128]{3,2,1,0:T(4,128)} %reshape.123) | copy-start | bytes 18874372
  162.8 6.0 %slice-start = ((s8[6291456]{0:T(1024)(128)(4,1)}), s8[4194304]{0:T(1024)(128)(4,1)S(1)}, s32[]{:S(2)}) async-start(s8[6291456]{0:T(1024)(128)(4,1)} %bitcast.78), calls=%async_computation.2 | async-start | bytes 8388608
  167.7 1.6 slice-start.1
  173.6 2.7 copy-start.1
  176.3 7.6 %copy-start.8 = (s32[1,4]{1,0:T(1,128)S(1)}, s32[1,4]{1,0:T(1,128)}, u32[]{:S(2)}) copy-start(s32[1,4]{1,0:T(1,128)} %param.13) | copy-start | bytes 52
  178.4 24.0 %collective-permute-start.2 = (f32[128,7,512]{2,0,1:T(8,128)}, f32[128,7,512]{2,0,1:T(8,128)S(1)}, u32[]{:S(2)}, u32[]{:S(2)}) collective-permute-start(f32[128,7,512]{2,0,1:T(8,128)} %get-tuple-element.13), channel_id=1, source_target_pairs={{0,1},{1,2},{2,3},{3,4},{4,5},{5,6},{6,7},{7,8},{8,9},{9,10},{10,1... | collective-permute-start | bytes 5505032 | tf_op jit(solution)/shard_map/ppermute | solution.py:17
  182.0 24.9 %collective-permute-start.3 = (f32[128,7,512]{2,0,1:T(8,128)}, f32[128,7,512]{2,0,1:T(8,128)}, u32[]{:S(2)}, u32[]{:S(2)}) collective-permute-start(f32[128,7,512]{2,0,1:T(8,128)} %get-tuple-element.14), channel_id=1, source_target_pairs={{1,0},{2,1},{3,2},{4,3},{5,4},{6,5},{7,6},{8,7},{9,8},{10,9},{11,1... | collective-permute-start | bytes 5505032 | tf_op jit(solution)/shard_map/ppermute | solution.py:19
  291.4 6.5 %copy-start.2 = (f32[128,24,4,128]{3,2,1,0:T(4,128)S(1)}, f32[128,24,4,128]{3,2,1,0:T(4,128)}, u32[]{:S(2)}) copy-start(f32[128,24,4,128]{3,2,1,0:T(4,128)} %reshape.128) | copy-start | bytes 18874372
Sparse Core Ops, SparseCore 0:
  316.1 225.9 all-gather.1
